TPU v7x, 1024 devices: a whole 4x4x32 slice. The times are simulated.
1024 devices in a mesh: replica: 64 (over y_lo, z), shard: 16 (over x, y_hi, core).
Axes of the slice: x: 4, y: 4 (y_hi: 2, y_lo: 2; y = y_hi * 2 + y_lo), z: 32, core: 2. Of those that a mesh axis runs over, the one named last changes fastest.
Arguments:
- features: bfloat16 [16384, 4096], P('replica', 'shard'), may hold values from -6 to 6
- weight: bfloat16 [128, 1024, 128], P('shard'), may hold values from -0.1875 to 0.1875
- rows_index: int32 [128, 8], replicated, may hold values from 0 to 31, as said below
- cotangent: bfloat16 [16384, 16384], P('replica', 'shard'), may hold values from -6 to 6
Outputs:
- activated: bfloat16 [16384, 16384], P('replica', 'shard')
- input_grad: bfloat16 [16384, 4096], P('replica', 'shard')
- weight_grad: float32 [128, 1024, 128], P('shard', 'replica')
Inputs may be any that keep to these rules, and one draw needn't show every extreme that they name: `rows_index`: each block column lists 8 different block rows.
All inputs are finite; a program needn't handle non-finite values.
Results may differ from a plain program's by a relative error of at most 0.02.
Values may be sent and summed in bfloat16 or wider, within the bound.
A program may use at most 64 MiB of HBM per device.

v0:
```python
import math

import jax
import jax.numpy as jnp
from jax import lax
from jax.sharding import PartitionSpec as P


def local(features, weight, rows_index, cotangent):
    tokens_here = features.shape[0]
    side = weight.shape[2]
    columns = weight.shape[0]
    per_column = weight.shape[1] // side
    scale = 1.0 / math.sqrt(tokens_here * lax.axis_size("replica"))
    whole = lax.all_gather(features, "shard", axis=1, tiled=True)
    block_rows = whole.shape[1] // side
    blocks = whole.reshape(tokens_here, block_rows, side)
    first = lax.axis_index("shard") * columns
    local_rows = lax.dynamic_slice_in_dim(rows_index, first, columns, 0)
    selected_rows = blocks[:, local_rows]
    block_weight_tiles = weight.reshape(columns, per_column, side, side)
    preactivation = jnp.einsum(
        "defv,efvp->dep", selected_rows, block_weight_tiles, preferred_element_type=jnp.float32
    )
    sig = jax.nn.sigmoid(preactivation)
    activated = (preactivation * sig).astype(jnp.bfloat16).reshape(tokens_here, columns * side)
    slope = (
        cotangent.astype(jnp.float32).reshape(tokens_here, columns, side)
        * sig
        * (1.0 + preactivation * (1.0 - sig))
    )
    output_difference = slope.astype(jnp.bfloat16)
    backward_result = jnp.einsum(
        "iov,omgv->iomg", output_difference, block_weight_tiles, preferred_element_type=jnp.float32
    )
    positions = jnp.arange(block_rows, dtype=jnp.int32)
    onehot = (local_rows[:, :, None] == positions[None, None, :]).astype(jnp.float32)
    partial_value = jnp.einsum("tckr,ckb->tbr", backward_result, onehot).reshape(
        tokens_here, block_rows * side
    )
    input_grad = lax.psum_scatter(
        partial_value.astype(jnp.bfloat16), "shard", scatter_dimension=1, tiled=True
    )
    shard_gradient = jnp.einsum(
        "qlpf,qlx->lpfx", selected_rows, output_difference, preferred_element_type=jnp.float32
    )
    shard_gradient = shard_gradient.reshape(columns, per_column * side, side)
    weight_grad = (
        lax.psum_scatter(shard_gradient, "replica", scatter_dimension=1, tiled=True) * scale
    )
    return (activated, input_grad, weight_grad)


def solution(mesh):
    placed = (P("replica", "shard"), P("shard", None, None), P(), P("replica", "shard"))
    return jax.shard_map(
        local,
        mesh=mesh,
        in_specs=placed,
        out_specs=(P("replica", "shard"), P("replica", "shard"), P("shard", "replica", None)),
        check_vma=False,
    )
```

profile of v0, /device:TPU:6, one launch (start us, length us, event | category | flops | bytes accessed | tf_op | source)
XLA Modules:
  0.0 519.2 jit_solution(8933484811972014050)
XLA Ops:
  7.2 0.0 copy-start
  7.2 0.0 all-gather.2.cloned.1.call-start
  7.2 1.8 copy.23
  9.0 0.0 all-gather.2.cloned.1.call-update
  9.1 0.0 reduce-scatter.5.cloned.1.call-start
  9.1 0.8 compare_select_fusion
  9.9 0.1 copy.24
  9.9 0.1 reshape.37
  10.0 2.3 copy.30
  12.3 92.2 %all-gather.2.cloned.1.call-done = bf16[256,4096]{0,1:T(8,128)(2,1)} async-done(((bf16[256,256]{0,1:T(8,128)(2,1)}), bf16[256,4096]{0,1:T(8,128)(2,1)}) %all-gather.2.cloned.1.call-update) | async-done | bytes 2097168 | tf_op jit(solution)/shard_map/all_gather | solution.py:15
  104.6 4.1 copy.25
  108.6 4.6 gather_fusion
  113.3 6.5 %copy.26 = bf16[8,8,256,128]{2,3,1,0:T(8,128)(2,1)} copy(bf16[8,8,256,128]{3,2,1,0:T(8,128)(2,1)} %bitcast.43) | data formatting | bytes 8388608 | tf_op jit(solution)/shard_map/gather | solution.py:20
  119.7 0.0 copy-done
  119.7 0.0 copy-start.1
  119.7 4.3 multiply_convert_fusion
  124.1 0.0 copy-done.1
  124.1 3.2 fusion.2
  127.3 0.0 reduce-scatter.5.cloned.1.call-update
  127.3 0.0 reduce-scatter.3.cloned.1.call-start
  127.4 0.1 copy.29
  127.4 1.3 convolution_bitcast_fusion
  128.7 3.0 bitcast_convert_fusion
  131.7 2.3 copy.53
  134.0 0.0 reduce-scatter.3.cloned.1.call-update
  134.1 1.0 copy.34
  135.1 264.9 %reduce-scatter.5.cloned.1.call-done = f32[8,16,128]{2,1,0:T(8,128)} async-done(((f32[8,1024,128]{2,1,0:T(8,128)}), f32[8,16,128]{2,1,0:T(8,128)}) %reduce-scatter.5.cloned.1.call-update) | async-done | bytes 65552 | tf_op jit(solution)/shard_map/reduce_scatter | solution.py:49
  400.0 1.5 broadcast_multiply_fusion
  401.5 111.2 %reduce-scatter.3.cloned.1.call-done = bf16[256,256]{1,0:T(8,128)(2,1)} async-done(((bf16[256,4096]{1,0:T(8,128)(2,1)}), bf16[256,256]{1,0:T(8,128)(2,1)}) %reduce-scatter.3.cloned.1.call-update) | async-done | bytes 131088 | tf_op jit(solution)/shard_map/reduce_scatter | solution.py:41
  (1 shorter events, 0.0 us)
Async XLA Ops:
  7.2 112.6 %copy-start = (bf16[8,1024,128]{2,1,0:T(8,128)(2,1)S(1)}, bf16[8,1024,128]{2,1,0:T(8,128)(2,1)}, u32[]{:S(2)}) copy-start(bf16[8,1024,128]{2,1,0:T(8,128)(2,1)} %param.5) | copy-start | bytes 6291460
  7.2 97.4 %all-gather.2.cloned.1.call-start = ((), (), s32[]{:S(2)}) async-start(), calls=%async_computation.2 | async-start | bytes 2228224 | tf_op jit(solution)/shard_map/all_gather | solution.py:15
  9.1 390.9 %reduce-scatter.5.cloned.1.call-start = ((), (), s32[]{:S(2)}) async-start(), calls=%async_computation.4 | async-start | bytes 4259840 | tf_op jit(solution)/shard_map/reduce_scatter | solution.py:49
  119.7 4.3 copy-start.1
  127.3 385.4 %reduce-scatter.3.cloned.1.call-start = ((), (), s32[]{:S(2)}) async-start(), calls=%async_computation.3 | async-start | bytes 2228224 | tf_op jit(solution)/shard_map/reduce_scatter | solution.py:41
Sparse Core Ops, SparseCore 0:
  13.0 91.5 all-gather.1
  127.4 272.5 reduce-scatter.4
  407.6 105.0 reduce-scatter.2
where the time goes:
time: 520 us; the launch traced here: 519 us
  waiting for transfers between devices  468 us (90%)
  local copies, waits for them, and re-layouts  22.8 us (4%)
  between operations  13.8 us (3%)
  matrix products  11.8 us (2%)
    reduce_scatter x1, waiting for transfers between devices, local(): lax.psum_scatter(shard_gradient, 'replica', scatter_dimension=1, tiled=True)  265 us
    reduce_scatter x1, waiting for transfers between devices, local(): lax.psum_scatter(partial_value.astype(jnp.bfloat16), 'shard', scatter_dim...  111 us
    all_gather x1, waiting for transfers between devices, local(): whole = lax.all_gather(features, 'shard', axis=1, tiled=True)  92.2 us
    gather x2, local copies, waits for them, and re-layouts, local(): selected_rows = blocks[:, local_rows]  11.1 us
  transfers between devices with their start and end apart: 3, of which 3 were waited for; matrix products, arithmetic and copies ran while one was open for 2% of the time, Pallas kernels for 0%

commit v1 on v0

v1 whole, which is shorter than its diff:
```python
import math

import jax
import jax.numpy as jnp
from jax import lax
from jax.experimental import pallas as pl
from jax.experimental.pallas import tpu as pltpu
from jax.sharding import PartitionSpec as P

MESH = pl.DeviceIdType.MESH
F32, BF16 = jnp.float32, jnp.bfloat16
NX, NZ = 4, 32
NG = 2


def dot_nn(a, b):
    return lax.dot_general(a, b, (((1,), (0,)), ((), ())), preferred_element_type=F32)


def dot_nt(a, b):
    return lax.dot_general(a, b, (((1,), (1,)), ((), ())), preferred_element_type=F32)


def kernel(
    rows, feat, w_hbm, cot_hbm,
    act_out, ig_out, wg_out,
    xt, wz, wt, wd, cot, cott, dt, xs, act, own,
    zsend, zrecv, ysend, yrecv, csend, crecv, gsend, grecv, gown,
    local_sem, act_sem, ag_s, ag_r, z_s, z_r, y_s, y_r, c_s, c_r, g_s, g_r,
):
    tokens = feat.shape[0]
    ncol = wt.shape[0]
    per_group = ncol // NG
    r = lax.axis_index("replica")
    s = lax.axis_index("shard")
    ylo, z = r // NZ, r % NZ
    x, yh, core = s // 4, (s // 2) % 2, s % 2

    def shard_at(dx, dy, dc):
        return ((x + dx) % NX) * 4 + ((yh + dy) % 2) * 2 + (core + dc) % 2

    def dev_shard(dx, dy, dc):
        return {"replica": r, "shard": shard_at(dx, dy, dc)}

    def dev_z(step):
        return {"replica": ylo * NZ + (z + step + NZ) % NZ, "shard": s}

    dev_y = {"replica": (1 - ylo) * NZ + z, "shard": s}
    offsets = [(dx, dy) for dy in (0, 1) for dx in (0, 1, 3, 2)]

    w_copy = pltpu.make_async_copy(w_hbm, wz.at[pl.ds(0, w_hbm.shape[0])], local_sem.at[0])
    w_copy.start()
    cot_copy = pltpu.make_async_copy(cot_hbm, cot, local_sem.at[1])
    cot_copy.start()

    barrier = pltpu.get_barrier_semaphore()
    peers = [dev_shard(dx, dy, 0) for dx, dy in offsets[1:]] + [dev_shard(0, 0, 1), dev_z(1), dev_z(-1), dev_y]
    for peer in peers:
        pl.semaphore_signal(barrier, inc=1, device_id=peer, device_id_type=MESH)

    mine = feat[...].T.reshape(2, feat.shape[1] // 2, tokens)
    xt[pl.ds(2 * s, 2)] = mine
    pl.semaphore_wait(barrier, len(peers))

    sends = []

    def remote(src, dst, send_sem, recv_sem, device):
        return pltpu.make_async_remote_copy(
            src_ref=src, dst_ref=dst, send_sem=send_sem, recv_sem=recv_sem,
            device_id=device, device_id_type=MESH,
        )

    def push(*args):
        copy = remote(*args)
        copy.start()
        sends.append(copy)

    right, left = dev_shard(1, 0, 0), dev_shard(3, 0, 0)
    across, sibling = dev_shard(0, 1, 0), dev_shard(0, 0, 1)

    def half(dx, dy, h):
        return xt.at[2 * shard_at(dx, dy, 0) + h]

    def block(dx, dy, dc=0):
        return xt.at[pl.ds(2 * shard_at(dx, dy, dc), 2)]

    def gather_send(m, ref, device):
        push(ref, ref, ag_s.at[m], ag_r.at[m], device)

    def gather_wait(m, ref):
        remote(ref, ref, ag_s.at[m], ag_r.at[m], sibling).wait_recv()

    gather_send(0, half(0, 0, 0), right)
    gather_send(3, half(0, 0, 1), left)
    gather_send(4, half(0, 0, 0), across)
    gather_send(5, half(0, 0, 1), across)
    gather_send(1, half(0, 0, 1), right)
    gather_send(2, half(0, 0, 0), left)
    gather_send(14, block(0, 0), sibling)

    def transpose_cot():
        cot_copy.wait()
        for c in range(ncol):
            cott[c] = cot[:, c * 128 : (c + 1) * 128].T

    def transpose_w(c):
        wt[c] = wz[pl.ds(8 * c, 8)].reshape(8 * 128, 128).T

    def dense_w(c):
        listed = [rows[k, s * ncol + c] for k in range(8)]

        def body(b, carry):
            index = 8 * ncol
            for k in range(8):
                index = jnp.where(listed[k] == b, 8 * c + k, index)
            wd[b, :, c * 128 : (c + 1) * 128] = wz[index]
            return carry

        lax.fori_loop(0, 32, body, 0)

    w_copy.wait()
    wz[8 * ncol] = jnp.zeros((128, 128), BF16)
    transpose_w(0)
    transpose_w(1)

    gather_wait(0, half(3, 0, 0))
    gather_send(6, half(3, 0, 0), right)
    gather_wait(3, half(1, 0, 1))
    gather_send(7, half(1, 0, 1), left)
    transpose_w(2)
    transpose_w(3)
    gather_wait(4, half(0, 1, 0))
    gather_send(8, half(0, 1, 0), right)
    gather_send(10, half(0, 1, 0), left)
    gather_wait(5, half(0, 1, 1))
    gather_send(11, half(0, 1, 1), left)
    gather_send(9, half(0, 1, 1), right)
    gather_send(17, block(0, 1), sibling)
    gather_wait(1, half(3, 0, 1))
    gather_send(15, block(3, 0), sibling)
    gather_wait(2, half(1, 0, 0))
    gather_send(16, block(1, 0), sibling)
    for c in range(4, ncol):
        transpose_w(c)
    gather_wait(6, half(2, 0, 0))
    gather_wait(7, half(2, 0, 1))
    gather_send(18, block(2, 0), sibling)
    transpose_cot()
    gather_wait(8, half(3, 1, 0))
    gather_send(12, half(3, 1, 0), right)
    gather_wait(11, half(1, 1, 1))
    gather_send(13, half(1, 1, 1), left)
    gather_wait(9, half(3, 1, 1))
    gather_send(19, block(3, 1), sibling)
    gather_wait(10, half(1, 1, 0))
    gather_send(20, block(1, 1), sibling)
    dense_w(0)
    dense_w(1)
    gather_wait(12, half(2, 1, 0))
    gather_wait(13, half(2, 1, 1))
    gather_send(21, block(2, 1), sibling)
    for m, (dx, dy) in zip(range(14, 22), ((0, 0), (3, 0), (1, 0), (0, 1), (2, 0), (3, 1), (1, 1), (2, 1))):
        gather_wait(m, block(dx, dy, 1))

    act_copies = []

    def column(c):
        for k in range(8):
            xs[c % 2, k * 128 : (k + 1) * 128, :] = xt[rows[k, s * ncol + c]]
        pre = dot_nn(wt[c], xs[c % 2])
        sig = jax.nn.sigmoid(pre)
        act[:, c * 128 : (c + 1) * 128] = (pre * sig).T.astype(BF16)
        slope = cott[c].astype(F32) * sig * (1.0 + pre * (1.0 - sig))
        dt[c * 128 : (c + 1) * 128, :] = slope.astype(BF16)
        grad = dot_nt(xs[c % 2], dt[c * 128 : (c + 1) * 128, :])
        own[c] = grad.reshape(2, NZ, 16, 128)

    top = (NZ // 2, NZ // 2 - 1)
    sign = (1, -1)

    def own_part(g, owner):
        return own[per_group * g : per_group * (g + 1), :, owner]

    def z_wait(g, d, n):
        remote(zsend.at[g, d, n], zrecv.at[g, d, n], z_s.at[g, d, n], z_r.at[g, d, n], sibling).wait_recv()

    def ring(g, j):
        for d in (0, 1):
            n = top[d] - j
            if n < 1:
                continue
            total = own_part(g, (z + sign[d] * n + NZ) % NZ)
            if j > 0:
                z_wait(g, d, n)
                total = total + zrecv[g, d, n].astype(F32)
            zsend[g, d, n] = total.astype(BF16)
            push(zsend.at[g, d, n], zrecv.at[g, d, n - 1], z_s.at[g, d, n], z_r.at[g, d, n - 1], dev_z(sign[d]))

    def ring_end(g):
        z_wait(g, 1, 0)
        z_wait(g, 0, 0)
        low = per_group * g
        other = own[low : low + per_group, 1 - ylo, z]
        for d in (0, 1):
            other = other + zrecv[g, d, 0, :, 1 - ylo].astype(F32)
        ysend[g] = other.astype(BF16)
        push(ysend.at[g], yrecv.at[g], y_s.at[g], y_r.at[g], dev_y)

    def finish(g, scale):
        low = per_group * g
        total = own[low : low + per_group, ylo, z]
        for d in (0, 1):
            total = total + zrecv[g, d, 0, :, ylo].astype(F32)
        remote(ysend.at[g], yrecv.at[g], y_s.at[g], y_r.at[g], dev_y).wait_recv()
        wg_out[low : low + per_group] = (total + yrecv[g].astype(F32)) * scale

    def partial(dx, dy, dc):
        weights = wd[pl.ds(2 * shard_at(dx, dy, dc), 2)].reshape(256, ncol * 128)
        return dot_nn(weights, dt[...])

    def sibling_task(p):
        dx, dy = offsets[p]
        csend[p] = partial(dx, dy, 1).astype(BF16)
        push(csend.at[p], crecv.at[p], c_s.at[p], c_r.at[p], sibling)

    def chip_task(p):
        dx, dy = offsets[p]
        total = partial(dx, dy, 0)
        remote(csend.at[p], crecv.at[p], c_s.at[p], c_r.at[p], sibling).wait_recv()
        total = total + crecv[p].astype(F32)
        if p == 0:
            gown[...] = total
            return
        gsend[p - 1] = total.astype(BF16)
        push(gsend.at[p - 1], grecv.at[p - 1], g_s.at[p - 1], g_r.at[p - 1], dev_shard(dx, dy, 0))

    def gather_grad():
        total = gown[...]
        for p in range(1, 8):
            remote(gsend.at[p - 1], grecv.at[p - 1], g_s.at[p - 1], g_r.at[p - 1], sibling).wait_recv()
            total = total + grecv[p - 1].astype(F32)
        ig_out[...] = total.T.astype(BF16)

    steps = NZ // 2
    tasks = [lambda p=p: sibling_task(p) for p in (7, 6, 5, 4, 3, 2, 1, 0)]
    tasks += [lambda p=p: chip_task(p) for p in (7, 6, 5, 4, 3, 2, 1, 0)]
    tasks = [lambda c=c: dense_w(c) for c in range(2, ncol)] + tasks
    todo = [0] * NG
    for c in range(ncol):
        column(c)
        for g in range(NG):
            if (c + 1) >= per_group * (g + 1) and todo[g] < steps:
                ring(g, todo[g])
                todo[g] += 1
    act_copy = pltpu.make_async_copy(act, act_out, act_sem)
    act_copy.start()
    while min(todo) < steps:
        for g in range(NG):
            if todo[g] < steps:
                if tasks:
                    tasks.pop(0)()
                ring(g, todo[g])
                todo[g] += 1
    while tasks:
        tasks.pop(0)()
    for g in range(NG):
        ring_end(g)
    gather_grad()
    scale = 1.0 / math.sqrt(tokens * lax.axis_size("replica"))
    for g in range(NG):
        finish(g, scale)
    for copy in sends:
        copy.wait_send()
    act_copy.wait()


def local(features, weight, rows_index, cotangent):
    tokens, width = features.shape
    columns, depth, side = weight.shape
    blocks = columns * depth // side
    per_group = columns // NG
    dma = pltpu.SemaphoreType.DMA
    vmem = pl.BlockSpec(memory_space=pltpu.VMEM)
    anywhere = pl.BlockSpec(memory_space=pl.ANY)
    return pl.pallas_call(
        kernel,
        out_shape=(
            jax.ShapeDtypeStruct((tokens, columns * side), BF16),
            jax.ShapeDtypeStruct((tokens, width), BF16),
            jax.ShapeDtypeStruct((columns, 16, side), F32),
        ),
        in_specs=[pl.BlockSpec(memory_space=pltpu.SMEM), vmem, anywhere, anywhere],
        out_specs=(anywhere, vmem, vmem),
        scratch_shapes=[
            pltpu.VMEM((32, side, tokens), BF16),
            pltpu.VMEM((blocks + 1, side, side), BF16),
            pltpu.VMEM((columns, side, depth), BF16),
            pltpu.VMEM((32, side, columns * side), BF16),
            pltpu.VMEM((tokens, columns * side), BF16),
            pltpu.VMEM((columns, side, tokens), BF16),
            pltpu.VMEM((columns * side, tokens), BF16),
            pltpu.VMEM((2, depth, tokens), BF16),
            pltpu.VMEM((tokens, columns * side), BF16),
            pltpu.VMEM((columns, 2, NZ, 16, side), F32),
            pltpu.VMEM((NG, 2, NZ // 2 + 1, per_group, 2, 16, side), BF16),
            pltpu.VMEM((NG, 2, NZ // 2 + 1, per_group, 2, 16, side), BF16),
            pltpu.VMEM((NG, per_group, 16, side), BF16),
            pltpu.VMEM((NG, per_group, 16, side), BF16),
            pltpu.VMEM((8, 2 * side, tokens), BF16),
            pltpu.VMEM((8, 2 * side, tokens), BF16),
            pltpu.VMEM((7, 2 * side, tokens), BF16),
            pltpu.VMEM((7, 2 * side, tokens), BF16),
            pltpu.VMEM((2 * side, tokens), F32),
            dma((2,)), dma,
            dma((22,)), dma((22,)),
            dma((NG, 2, NZ // 2 + 1)), dma((NG, 2, NZ // 2 + 1)),
            dma((NG,)), dma((NG,)),
            dma((8,)), dma((8,)),
            dma((7,)), dma((7,)),
        ],
        compiler_params=pltpu.CompilerParams(
            collective_id=0, has_side_effects=True, vmem_limit_bytes=56 * 2**20
        ),
        name="fused",
    )(rows_index.T, features, weight.reshape(blocks, side, side), cotangent)


def solution(mesh):
    placed = (P("replica", "shard"), P("shard", None, None), P(), P("replica", "shard"))
    return jax.shard_map(
        local,
        mesh=mesh,
        in_specs=placed,
        out_specs=(P("replica", "shard"), P("replica", "shard"), P("shard", "replica", None)),
        check_vma=False,
    )
```

time: 520 us -> 113 us (0.22)
  waiting for transfers between devices: 468 us -> 0 us
  Pallas kernels: 0 us -> 107 us
  local copies, waits for them, and re-layouts: 22.8 us -> 4.91 us
  between operations: 13.8 us -> 0.64 us
  matrix products: 11.8 us -> 0 us
    reduce_scatter x2 -> x0, waiting for transfers between devices: 376 us -> none  [the longest x1 265 us: local(): lax.psum_scatter(shard_gradient, 'replica', scatter_dimension=1, tiled=True)]
    pallas_call x0 -> x1, Pallas kernels: none -> 107 us  [local(): pl.pallas_call(kernel, out_shape=(jax.ShapeDtypeStruct((tokens, columns *...]
    all_gather x1 -> x0, waiting for transfers between devices: 92.2 us -> none  [local(): whole = lax.all_gather(features, 'shard', axis=1, tiled=True)]
    dot_general x4 -> x0, matrix products: 11.8 us -> none  [the longest x1 4.33 us: local(): jnp.einsum('defv,efvp->dep', selected_rows, block_weight_tiles, preferred...]
    gather x2 -> x0, local copies, waits for them, and re-layouts: 11.1 us -> none  [local(): selected_rows = blocks[:, local_rows]]
    reshape x2 -> x0, local copies, waits for them, and re-layouts: 6.36 us -> none  [the longest x1 4.06 us: local(): blocks = whole.reshape(tokens_here, block_rows, side)]
  transfers between devices with their start and end apart: 3 -> 0, of which waited for: 3 -> 0; matrix products, arithmetic and copies ran while one was open for 2% -> 0% of each run, Pallas kernels for 0% -> 0%
where the time goes in v1:
time: 113 us
  Pallas kernels  107 us (95%)
  local copies, waits for them, and re-layouts  4.91 us (4%)
    pallas_call x1, Pallas kernels, local(): pl.pallas_call(kernel, out_shape=(jax.ShapeDtypeStruct((tokens, columns *...  107 us
    unnamed x3, local copies, waits for them, and re-layouts  4.91 us

profile of v1, /device:TPU:6, one launch (start us, length us, event | category | flops | bytes accessed | tf_op | source)
XLA Modules:
  0.0 112.6 jit_solution(7631065022557171583)
XLA Ops:
  0.6 107.1 %fused.1 = (bf16[256,1024]{1,0:T(8,128)(2,1)}, bf16[256,256]{1,0:T(8,128)(2,1)}, f32[8,16,128]{2,1,0:T(8,128)}) custom-call(s32[8,128]{1,0:T(8,128)} %bitcast.3, bf16[256,256]{1,0:T(8,128)(2,1)} %feat.1, bf16[64,128,128]{2,1,0:T(8,128)(2,1)} %bitcast.2, bf16[256,1024]{1,0:T(8,128)(2,1)} %cot_hbm.1), custom_call_target="tpu_custom_call" | custom-call | tf_op jit(solution)/shard_map/fused/pallas_call | solution.py:285
  107.7 1.9 %copy.10 = bf16[256,1024]{1,0:T(8,128)(2,1)} copy(bf16[256,1024]{1,0:T(8,128)(2,1)} %get-tuple-element.6) | data formatting | bytes 1048576
  109.6 1.6 %copy.11 = bf16[256,256]{1,0:T(8,128)(2,1)} copy(bf16[256,256]{1,0:T(8,128)(2,1)} %get-tuple-element.7) | data formatting | bytes 262144
  111.1 1.5 %copy.12 = f32[8,16,128]{2,1,0:T(8,128)} copy(f32[8,16,128]{2,1,0:T(8,128)} %get-tuple-element.8) | data formatting | bytes 131072

commit v2 on v1

v2 whole, which is shorter than its diff:
```python
import math

import jax
import jax.numpy as jnp
from jax import lax
from jax.experimental import pallas as pl
from jax.experimental.pallas import tpu as pltpu
from jax.sharding import PartitionSpec as P

MESH = pl.DeviceIdType.MESH
F32, BF16 = jnp.float32, jnp.bfloat16
NX, NZ = 4, 32


def dot_nn(a, b):
    return lax.dot_general(a, b, (((1,), (0,)), ((), ())), preferred_element_type=F32)


def dot_nt(a, b):
    return lax.dot_general(a, b, (((1,), (1,)), ((), ())), preferred_element_type=F32)


NB = 4
PARENT = (-1, 0, 1, 2, 0, 4, 5, 6, 4, 8, 9, 10, 8, 12, 12, 14)


def hop(e):
    return e - PARENT[e]


def children(e, top):
    return [child for child in range(top) if PARENT[child] == e]


def kernel(
    rows, feat, w_hbm, cot_hbm,
    act_out, ig_out, wg_out,
    xt, wz, wt, wd, cot, cott, dt, xs, act, own,
    asend, arecv, bsend, brecv, ysend, yrecv, fsend, frecv, csend, crecv, gsend, grecv, gown,
    local_sem, act_sem, ag_s, ag_r, a_s, a_r, b_s, b_r, y_s, y_r, f_s, f_r, c_s, c_r, g_s, g_r,
):
    tokens = feat.shape[0]
    ncol = wt.shape[0]
    r = lax.axis_index("replica")
    s = lax.axis_index("shard")
    ylo, z = r // NZ, r % NZ
    x, yh, core = s // 4, (s // 2) % 2, s % 2
    top = (NZ // 2, NZ // 2 - 1)
    sign = (1, -1)

    def shard_at(dx, dy, dc):
        return ((x + dx) % NX) * 4 + ((yh + dy) % 2) * 2 + (core + dc) % 2

    def dev_shard(dx, dy, dc):
        return {"replica": r, "shard": shard_at(dx, dy, dc)}

    def dev_z(step):
        return {"replica": ylo * NZ + (z + step + NZ) % NZ, "shard": s}

    dev_y = {"replica": (1 - ylo) * NZ + z, "shard": s}
    sibling = dev_shard(0, 0, 1)
    others = ((2, 1), (1, 1), (3, 1), (2, 0), (0, 1), (1, 0), (3, 0))

    w_copy = pltpu.make_async_copy(w_hbm, wz.at[pl.ds(0, w_hbm.shape[0])], local_sem.at[0])
    w_copy.start()
    cot_copy = pltpu.make_async_copy(cot_hbm, cot, local_sem.at[1])
    cot_copy.start()

    barrier = pltpu.get_barrier_semaphore()
    peers = [dev_shard(dx, dy, 0) for dx, dy in others] + [sibling, dev_y]
    peers += [dev_z(d * h) for h in sorted({hop(e) for e in range(len(PARENT))}) for d in sign]
    for peer in peers:
        pl.semaphore_signal(barrier, inc=1, device_id=peer, device_id_type=MESH)

    mine = feat[...].T.reshape(2, feat.shape[1] // 2, tokens)
    xt[pl.ds(2 * s, 2)] = mine
    pl.semaphore_wait(barrier, len(peers))

    sends = []

    def remote(src, dst, send_sem, recv_sem, device):
        return pltpu.make_async_remote_copy(
            src_ref=src, dst_ref=dst, send_sem=send_sem, recv_sem=recv_sem,
            device_id=device, device_id_type=MESH,
        )

    def push(*args):
        copy = remote(*args)
        copy.start()
        sends.append(copy)

    right, left = dev_shard(1, 0, 0), dev_shard(3, 0, 0)
    across = dev_shard(0, 1, 0)

    def half(dx, dy, h):
        return xt.at[2 * shard_at(dx, dy, 0) + h]

    def block(dx, dy, dc=0):
        return xt.at[pl.ds(2 * shard_at(dx, dy, dc), 2)]

    def gather_send(m, ref, device):
        push(ref, ref, ag_s.at[m], ag_r.at[m], device)

    def gather_wait(m, ref):
        remote(ref, ref, ag_s.at[m], ag_r.at[m], sibling).wait_recv()

    gather_send(0, half(0, 0, 0), right)
    gather_send(3, half(0, 0, 1), left)
    gather_send(4, half(0, 0, 0), across)
    gather_send(5, half(0, 0, 1), across)
    gather_send(1, half(0, 0, 1), right)
    gather_send(2, half(0, 0, 0), left)
    gather_send(14, block(0, 0), sibling)

    def transpose_cot():
        cot_copy.wait()
        for c in range(ncol):
            cott[c] = cot[:, c * 128 : (c + 1) * 128].T

    def transpose_w(c):
        for part, first in ((0, ylo), (1, 1 - ylo)):
            four = wz[pl.ds(8 * c + 4 * first, 4)].reshape(4 * 128, 128)
            wt[c, :, part * 512 : (part + 1) * 512] = four.T

    def dense_w(c):
        listed = [rows[k, s * ncol + c] for k in range(8)]

        def body(b, carry):
            index = 8 * ncol
            for k in range(8):
                index = jnp.where(listed[k] == b, 8 * c + k, index)
            wd[b, :, c * 128 : (c + 1) * 128] = wz[index]
            return carry

        lax.fori_loop(0, 32, body, 0)

    w_copy.wait()
    wz[8 * ncol] = jnp.zeros((128, 128), BF16)
    transpose_w(0)
    transpose_w(1)

    gather_wait(0, half(3, 0, 0))
    gather_send(6, half(3, 0, 0), right)
    gather_wait(3, half(1, 0, 1))
    gather_send(7, half(1, 0, 1), left)
    transpose_w(2)
    transpose_w(3)
    gather_wait(4, half(0, 1, 0))
    gather_send(8, half(0, 1, 0), right)
    gather_send(10, half(0, 1, 0), left)
    gather_wait(5, half(0, 1, 1))
    gather_send(11, half(0, 1, 1), left)
    gather_send(9, half(0, 1, 1), right)
    gather_send(17, block(0, 1), sibling)
    gather_wait(1, half(3, 0, 1))
    gather_send(15, block(3, 0), sibling)
    gather_wait(2, half(1, 0, 0))
    gather_send(16, block(1, 0), sibling)
    for c in range(4, ncol):
        transpose_w(c)
    gather_wait(6, half(2, 0, 0))
    gather_wait(7, half(2, 0, 1))
    gather_send(18, block(2, 0), sibling)
    transpose_cot()
    gather_wait(8, half(3, 1, 0))
    gather_send(12, half(3, 1, 0), right)
    gather_wait(11, half(1, 1, 1))
    gather_send(13, half(1, 1, 1), left)
    gather_wait(9, half(3, 1, 1))
    gather_send(19, block(3, 1), sibling)
    gather_wait(10, half(1, 1, 0))
    gather_send(20, block(1, 1), sibling)
    gather_wait(12, half(2, 1, 0))
    gather_wait(13, half(2, 1, 1))
    gather_send(21, block(2, 1), sibling)
    for m, (dx, dy) in zip(range(14, 22), ((0, 0), (3, 0), (1, 0), (0, 1), (2, 0), (3, 1), (1, 1), (2, 1))):
        gather_wait(m, block(dx, dy, 1))

    def column(c):
        for j in range(8):
            xs[c % 2, j * 128 : (j + 1) * 128, :] = xt[rows[(4 * ylo + j) % 8, s * ncol + c]]
        pre = dot_nn(wt[c], xs[c % 2])
        sig = jax.nn.sigmoid(pre)
        act[:, c * 128 : (c + 1) * 128] = (pre * sig).T.astype(BF16)
        slope = cott[c].astype(F32) * sig * (1.0 + pre * (1.0 - sig))
        dt[c * 128 : (c + 1) * 128, :] = slope.astype(BF16)
        grad = dot_nt(xs[c % 2], dt[c * 128 : (c + 1) * 128, :])
        own[c] = grad.reshape(2, NZ, 16, 128)
        if c < NB:
            ysend[c] = own[c, 1].astype(BF16)
            push(ysend.at[c], yrecv.at[c], y_s.at[c], y_r.at[c], dev_y)

    def holder(send, recv, s_sem, r_sem, part):
        def wait(d, e):
            remote(send.at[d, e], recv.at[d, e], s_sem.at[d, e], r_sem.at[d, e], sibling).wait_recv()
            return recv[d, e].astype(F32)

        def relay(*distances):
            for e in distances:
                for d in (0, 1):
                    if e >= top[d]:
                        continue
                    total = part((z + sign[d] * (e + 1) + NZ) % NZ)
                    for child in children(e, top[d]):
                        total = total + wait(d, child)
                    send[d, e] = total.astype(BF16)
                    push(send.at[d, e], recv.at[d, e], s_sem.at[d, e], r_sem.at[d, e], dev_z(sign[d] * hop(e)))

        def end():
            return part(z) + wait(0, 0) + wait(1, 0)

        return relay, end

    a_relay, a_end = holder(asend, arecv, a_s, a_r, lambda owner: own[NB:, :, owner])
    b_relay, b_end = holder(
        bsend, brecv, b_s, b_r, lambda owner: own[:NB, 0, owner] + yrecv[:, owner].astype(F32)
    )

    def partial(dx, dy, dc):
        weights = wd[pl.ds(2 * shard_at(dx, dy, dc), 2)].reshape(256, ncol * 128)
        return dot_nn(weights, dt[...])

    def sibling_task(p):
        dx, dy = others[p] if p < 7 else (0, 0)
        csend[p] = partial(dx, dy, 1).astype(BF16)
        push(csend.at[p], crecv.at[p], c_s.at[p], c_r.at[p], sibling)

    def chip_task(p):
        dx, dy = others[p] if p < 7 else (0, 0)
        total = partial(dx, dy, 0)
        remote(csend.at[p], crecv.at[p], c_s.at[p], c_r.at[p], sibling).wait_recv()
        total = total + crecv[p].astype(F32)
        if p == 7:
            gown[...] = total
            return
        gsend[p] = total.astype(BF16)
        push(gsend.at[p], grecv.at[p], g_s.at[p], g_r.at[p], dev_shard(dx, dy, 0))

    def gather_grad():
        total = gown[...]
        for p in range(7):
            remote(gsend.at[p], grecv.at[p], g_s.at[p], g_r.at[p], sibling).wait_recv()
            total = total + grecv[p].astype(F32)
        ig_out[...] = total.T.astype(BF16)

    for c in range(ncol):
        column(c)
    act_copy = pltpu.make_async_copy(act, act_out, act_sem)
    act_copy.start()
    a_relay(15, 13, 11, 7, 3)
    for c in range(ncol):
        dense_w(c)
    a_relay(14, 10, 6, 2)
    for p in range(0, 4):
        sibling_task(p)
    for c in range(NB):
        remote(ysend.at[c], yrecv.at[c], y_s.at[c], y_r.at[c], dev_y).wait_recv()
    b_relay(15, 13)
    a_relay(12, 9, 5)
    b_relay(11, 7, 3)
    for p in range(4, 8):
        sibling_task(p)
    b_relay(14, 10, 6, 2)
    a_relay(1)
    for p in range(0, 3):
        chip_task(p)
    a_relay(8)
    b_relay(12, 9, 5)
    for p in range(3, 8):
        chip_task(p)
    a_relay(4)
    b_relay(8, 1)
    gather_grad()
    a_relay(0)
    b_relay(4)
    scale = 1.0 / math.sqrt(tokens * lax.axis_size("replica"))
    last = a_end()
    fsend[...] = last[:, 1].astype(BF16)
    push(fsend, frecv, f_s, f_r, dev_y)
    b_relay(0)
    remote(fsend, frecv, f_s, f_r, dev_y).wait_recv()
    wg_out[NB:] = (last[:, 0] + frecv[...].astype(F32)) * scale
    wg_out[:NB] = b_end() * scale
    for copy in sends:
        copy.wait_send()
    act_copy.wait()


def place(a, b, c, a_out, b_out, c_out):
    a_out[...] = a[...]
    b_out[...] = b[...]
    c_out[...] = c[...]


def local(features, weight, rows_index, cotangent):
    tokens, width = features.shape
    columns, depth, side = weight.shape
    blocks = columns * depth // side
    dma = pltpu.SemaphoreType.DMA
    vmem = pl.BlockSpec(memory_space=pltpu.VMEM)
    anywhere = pl.BlockSpec(memory_space=pl.ANY)
    shapes = (
        jax.ShapeDtypeStruct((tokens, columns * side), BF16),
        jax.ShapeDtypeStruct((tokens, width), BF16),
        jax.ShapeDtypeStruct((columns, 16, side), F32),
    )
    results = pl.pallas_call(
        kernel,
        out_shape=shapes,
        in_specs=[pl.BlockSpec(memory_space=pltpu.SMEM), vmem, anywhere, anywhere],
        out_specs=(anywhere, vmem, vmem),
        scratch_shapes=[
            pltpu.VMEM((32, side, tokens), BF16),
            pltpu.VMEM((blocks + 1, side, side), BF16),
            pltpu.VMEM((columns, side, depth), BF16),
            pltpu.VMEM((32, side, columns * side), BF16),
            pltpu.VMEM((tokens, columns * side), BF16),
            pltpu.VMEM((columns, side, tokens), BF16),
            pltpu.VMEM((columns * side, tokens), BF16),
            pltpu.VMEM((2, depth, tokens), BF16),
            pltpu.VMEM((tokens, columns * side), BF16),
            pltpu.VMEM((columns, 2, NZ, 16, side), F32),
            pltpu.VMEM((2, NZ // 2, columns - NB, 2, 16, side), BF16),
            pltpu.VMEM((2, NZ // 2, columns - NB, 2, 16, side), BF16),
            pltpu.VMEM((2, NZ // 2, NB, 16, side), BF16),
            pltpu.VMEM((2, NZ // 2, NB, 16, side), BF16),
            pltpu.VMEM((NB, NZ, 16, side), BF16),
            pltpu.VMEM((NB, NZ, 16, side), BF16),
            pltpu.VMEM((columns - NB, 16, side), BF16),
            pltpu.VMEM((columns - NB, 16, side), BF16),
            pltpu.VMEM((8, 2 * side, tokens), BF16),
            pltpu.VMEM((8, 2 * side, tokens), BF16),
            pltpu.VMEM((7, 2 * side, tokens), BF16),
            pltpu.VMEM((7, 2 * side, tokens), BF16),
            pltpu.VMEM((2 * side, tokens), F32),
            dma((2,)), dma,
            dma((22,)), dma((22,)),
            dma((2, NZ // 2)), dma((2, NZ // 2)),
            dma((2, NZ // 2)), dma((2, NZ // 2)),
            dma((NB,)), dma((NB,)),
            dma, dma,
            dma((8,)), dma((8,)),
            dma((7,)), dma((7,)),
        ],
        compiler_params=pltpu.CompilerParams(
            collective_id=0, has_side_effects=True, vmem_limit_bytes=56 * 2**20
        ),
        name="fused",
    )(rows_index.T, features, weight.reshape(blocks, side, side), cotangent)
    return pl.pallas_call(
        place,
        out_shape=shapes,
        in_specs=[vmem] * 3,
        out_specs=(vmem,) * 3,
        name="place",
    )(*results)


def solution(mesh):
    placed = (P("replica", "shard"), P("shard", None, None), P(), P("replica", "shard"))
    return jax.shard_map(
        local,
        mesh=mesh,
        in_specs=placed,
        out_specs=(P("replica", "shard"), P("replica", "shard"), P("shard", "replica", None)),
        check_vma=False,
    )
```

time: 113 us -> 87.9 us (0.78)
  Pallas kernels: 107 us -> 86.3 us
  local copies, waits for them, and re-layouts: 4.91 us -> 0 us
    pallas_call x1 -> x2, Pallas kernels: 107 us -> 86.3 us  [the longest x1 84.3 us: local(): pl.pallas_call(kernel, out_shape=shapes, in_specs=[pl.BlockSpec(memory_sp...]
    unnamed x3 -> x0, local copies, waits for them, and re-layouts: 4.91 us -> none
where the time goes in v2:
time: 87.9 us; the launch traced here: 86.9 us
  Pallas kernels  86.3 us (98%)
    pallas_call x1, Pallas kernels, local(): pl.pallas_call(kernel, out_shape=shapes, in_specs=[pl.BlockSpec(memory_sp...  84.3 us
    pallas_call x1, Pallas kernels, local(): pl.pallas_call(place, out_shape=shapes, in_specs=[vmem] * 3, out_specs=(v...  1.97 us

profile of v2, /device:TPU:6, one launch (start us, length us, event | category | flops | bytes accessed | tf_op | source)
XLA Modules:
  0.0 86.9 jit_solution(4510660499625200703)
XLA Ops:
  0.6 84.3 %fused.1 = (bf16[256,1024]{1,0:T(8,128)(2,1)}, bf16[256,256]{1,0:T(8,128)(2,1)}, f32[8,16,128]{2,1,0:T(8,128)}) custom-call(s32[8,128]{1,0:T(8,128)} %bitcast.3, bf16[256,256]{1,0:T(8,128)(2,1)} %feat.1, bf16[64,128,128]{2,1,0:T(8,128)(2,1)} %bitcast.2, bf16[256,1024]{1,0:T(8,128)(2,1)} %cot_hbm.1), custom_call_target="tpu_custom_call" | custom-call | tf_op jit(solution)/shard_map/fused/pallas_call | solution.py:307
  85.0 2.0 %place.1 = (bf16[256,1024]{1,0:T(8,128)(2,1)}, bf16[256,256]{1,0:T(8,128)(2,1)}, f32[8,16,128]{2,1,0:T(8,128)}) custom-call(bf16[256,1024]{1,0:T(8,128)(2,1)} %get-tuple-element.6.a, bf16[256,256]{1,0:T(8,128)(2,1)} %get-tuple-element.7.b, f32[8,16,128]{2,1,0:T(8,128)} %get-tuple-element.8.c), custom_call_target="tpu_custom_call" | custom-call | tf_op jit(solution)/shard_map/place/pallas_call | solution.py:350
